TPU v7x, 128 devices: a whole 4x4x4 slice. The times are simulated.
128 devices in a mesh: sample: 4 (over z), marker: 32 (over y, x, core).
Axes of the slice: x: 4, y: 4, z: 4, core: 2. Of those that a mesh axis runs over, the one named last changes fastest.
Arguments:
- genotypes: bfloat16 [8192, 131072], P('sample', 'marker'), may hold values from -6 to 6
- phenotypes: float32 [16, 8192], P(None, 'sample'), may hold values from -6 to 6
- message: float32 [16, 131072], P(None, 'marker'), may hold values from -6 to 6
- probes: float32 [112, 131072], P(None, 'marker'), may hold values from -16 to 16
- inclusion: float32 [16], replicated, may hold values from 0.3 to 0.6
- slab_ratio: float32 [16], replicated, may hold values from 0.25 to 0.67
- input_precision: float32 [16], replicated, may hold values from 0.5 to 2
- noise_precision: float32 [16], replicated, may hold values from 4 to 16
Outputs:
- estimate: float32 [16, 131072], P(None, 'marker')
- lmmse_estimate: float32 [16, 131072], P(None, 'marker')
All inputs are finite; a program needn't handle non-finite values.
Results may differ from a plain program's by a relative error of at most 0.0013.
Values may be sent and summed in bfloat16 or wider, within the bound.
A program may use at most 128 MiB of HBM per device.

v0:
```python
import jax
import jax.numpy as jnp
from jax import lax
from jax.sharding import PartitionSpec as P

MARKERS = 131072
ITERS = 2


def denoise(signal, precision, shrink, logit_base):
    energy = shrink * precision * signal * signal
    weight = jax.nn.sigmoid(logit_base + 0.5 * energy)
    return (shrink * weight * signal, shrink * weight * (1.0 + (1.0 - weight) * energy))


def contract_rows(vectors, genotypes):
    return lax.dot_general(
        vectors, genotypes, (((1,), (1,)), ((), ())), preferred_element_type=jnp.float32
    )


def project(vectors_b, genotypes, offset):
    partial_value = contract_rows(vectors_b, genotypes)
    predicted = lax.psum(partial_value, "marker")
    if offset is not None:
        predicted = offset - predicted
    predicted_b = predicted.astype(jnp.bfloat16)
    widened = predicted_b.astype(jnp.float32)
    back_sum = jnp.dot(predicted_b, genotypes, preferred_element_type=jnp.float32)
    return (back_sum, jnp.sum(widened * widened, axis=1))


def per_device(
    genotypes, phenotypes, message, probes, inclusion, slab_ratio, input_precision, noise_precision
):
    people = genotypes.shape[0] * lax.axis_size("sample")
    traits = message.shape[0]
    copies = probes.shape[0] // traits + 1
    shrink = (slab_ratio / (1.0 + slab_ratio))[:, None]
    odds = jnp.log(inclusion / (1.0 - inclusion))[:, None]
    logit_base = odds + 0.5 * jnp.log(1.0 - shrink)
    first, slopes = denoise(message, input_precision[:, None], shrink, logit_base)
    first_slope = lax.psum(jnp.sum(slopes, axis=1), "marker") / MARKERS
    second_precision = input_precision * (1.0 - first_slope) / first_slope
    centre = (first - first_slope[:, None] * message) / (1.0 - first_slope)[:, None]
    start_back, unused_square = project(centre.astype(jnp.bfloat16), genotypes, phenotypes)
    start_back = lax.psum(start_back, "sample")
    start_res = noise_precision[:, None] / people * start_back
    scale_col = jnp.tile(noise_precision / people, copies)[:, None]
    prec_col = jnp.tile(second_precision, copies)[:, None]
    iterate = jnp.concatenate([centre, jnp.zeros(probes.shape, jnp.float32)], axis=0)
    residual = jnp.concatenate([start_res, probes], axis=0)
    direction = residual
    norm_start = lax.psum(jnp.sum(residual * residual, axis=1), "marker")
    norm_now = norm_start
    for iteration in range(ITERS):
        back_sum, square = project(direction.astype(jnp.bfloat16), genotypes, None)
        back_sum = lax.psum(back_sum, "sample")
        applied = scale_col * back_sum + prec_col * direction
        curvature = lax.psum(jnp.sum(direction * applied, axis=1), "marker")
        step_size = norm_now / curvature
        iterate = iterate + step_size[:, None] * direction
        if iteration + 1 < ITERS:
            residual = residual - step_size[:, None] * applied
            norm_next = lax.psum(jnp.sum(residual * residual, axis=1), "marker")
            beta_ratio = norm_next / norm_now
            direction = residual + beta_ratio[:, None] * direction
            norm_now = norm_next
    lmmse_estimate = iterate[:traits]
    probe_local = jnp.sum(
        jnp.sum(probes * iterate[traits:], axis=1).reshape(copies - 1, traits), axis=0
    )
    probe_dot = lax.psum(probe_local, "marker")
    probe_norm = jnp.sum(norm_start[traits:].reshape(copies - 1, traits), axis=0)
    second_slope = second_precision * probe_dot / (probe_norm + 1e-06)
    next_precision = second_precision * (1.0 - second_slope) / second_slope
    next_message = (lmmse_estimate - second_slope[:, None] * centre) / (1.0 - second_slope)[:, None]
    slab_var = slab_ratio / input_precision
    next_shrink = (slab_var * next_precision / (1.0 + slab_var * next_precision))[:, None]
    next_base = odds + 0.5 * jnp.log(1.0 - next_shrink)
    estimate, unused_slopes = denoise(next_message, next_precision[:, None], next_shrink, next_base)
    return (estimate, lmmse_estimate)


def solution(mesh):
    return jax.shard_map(
        per_device,
        mesh=mesh,
        in_specs=(
            P("sample", "marker"),
            P(None, "sample"),
            P(None, "marker"),
            P(None, "marker"),
            P(),
            P(),
            P(),
            P(),
        ),
        out_specs=(P(None, "marker"), P(None, "marker")),
        check_vma=False,
    )
```

profile of v0, /device:TPU:1, one launch (start us, length us, event | category | flops | bytes accessed | tf_op | source)
XLA Modules:
  0.0 946.0 jit_solution(1127837189394486947)
XLA Ops:
  7.2 0.0 all-reduce.9.cloned.1.call-start
  7.2 0.7 multiply_add_fusion.4
  7.9 0.7 mul.192
  8.6 1.3 multiply_reduce_fusion.4
  9.8 63.8 %psum.84 = f32[16]{0:T(128)S(1)} all-reduce(f32[16]{0:T(128)S(1)} %multiply_reduce_fusion.4), channel_id=1, replica_groups=mesh['sample'=4,'marker'=32] {'marker'}, use_global_device_ids=true, to_apply=%region_1.0 | all-reduce | flops 16 | bytes 128 | tf_op jit(solution)/shard_map/psum | solution.py:43
  73.6 0.7 multiply_divide_fusion.1
  74.3 1.1 subtract_divide_fusion
  75.4 0.0 copy-start.3
  75.4 10.9 %fusion.17 = f32[16,2048]{1,0:T(8,128)} fusion(bf16[2048,4096]{1,0:T(8,128)(2,1)} %param.8, f32[16,4096]{1,0:T(8,128)S(1)} %subtract_divide_fusion), kind=kOutput, calls=%fused_computation.33 | convolution fusion | flops 268500992 | bytes 17170432 | tf_op jit(solution)/shard_map/dot_general | solution.py:17
  86.3 0.0 all-reduce.9.cloned.1.call-update
  86.3 0.0 copy-start.6
  86.3 0.0 copy-start
  86.4 0.0 all-reduce.11.cloned.1.call-start
  86.4 102.7 %all-reduce.9.cloned.1.call-done = f32[16,2048]{1,0:T(8,128)} async-done(((f32[16,2048]{1,0:T(8,128)}), f32[16,2048]{1,0:T(8,128)}) %all-reduce.9.cloned.1.call-update) | async-done | bytes 131088 | tf_op jit(solution)/shard_map/psum | solution.py:24
  189.1 0.0 copy-done.3
  189.1 8.8 fusion.19
  197.9 0.0 all-reduce.11.cloned.1.call-update
  197.9 0.0 all-reduce.13.cloned.1.call-start
  198.0 0.0 copy-done.6
  198.0 39.8 %all-reduce.11.cloned.1.call-done = f32[16,4096]{1,0:T(8,128)} async-done(((f32[16,4096]{1,0:T(8,128)}), f32[16,4096]{1,0:T(8,128)}) %all-reduce.11.cloned.1.call-update) | async-done | bytes 262160 | tf_op jit(solution)/shard_map/psum | solution.py:47
  237.8 1.0 broadcast_multiply_fusion
  238.8 0.0 copy-done
  238.8 11.4 %fusion.3 = f32[128,2048]{1,0:T(8,128)S(1)} fusion(bf16[2048,4096]{1,0:T(8,128)(2,1)} %param.8, f32[112,4096]{1,0:T(8,128)S(1)} %copy-done, f32[16,4096]{1,0:T(8,128)S(1)} %broadcast_multiply_fusion), kind=kOutput, calls=%fused_computation.13 | convolution fusion | flops 2149580800 | bytes 19922944 | tf_op jit(solution)/shard_map/dot_general | solution.py:17
  250.2 134.0 %all-reduce.16 = bf16[128,2048]{1,0:T(8,128)(2,1)} all-reduce(f32[128,2048]{1,0:T(8,128)S(1)} %fusion.3), channel_id=1, replica_groups=mesh['sample'=4,'marker'=32] {'marker'}, use_global_device_ids=true, to_apply=%region_6.0 | all-reduce | flops 262144 | bytes 1572864 | tf_op jit(solution)/shard_map/psum | solution.py:24
  384.2 9.6 %fusion.24 = f32[128,4096]{1,0:T(8,128)} fusion(bf16[128,2048]{1,0:T(8,128)(2,1)} %all-reduce.16, bf16[2048,4096]{1,0:T(8,128)(2,1)} %param.8), kind=kOutput, calls=%fused_computation.52 | convolution fusion | flops 2147483648 | bytes 19398656 | tf_op jit(solution)/shard_map/dot_general | solution.py:29
  393.9 0.0 all-reduce.13.cloned.1.call-update
  393.9 0.0 all-reduce.15.cloned.1.call-start
  394.0 0.1 mul.210
  394.0 0.1 mul.207
  394.1 59.5 %all-reduce.13.cloned.1.call-done = f32[128,4096]{1,0:T(8,128)} async-done(((f32[128,4096]{1,0:T(8,128)}), f32[128,4096]{1,0:T(8,128)}) %all-reduce.13.cloned.1.call-update) | async-done | bytes 2097168 | tf_op jit(solution)/shard_map/psum | solution.py:58
  453.6 2.2 multiply_reduce_fusion.2
  455.8 62.9 %all-reduce.1 = (f32[128]{0:T(128)S(1)}, f32[128]{0:T(128)S(1)}) all-reduce(f32[128]{0:T(128)S(1)} %get-tuple-element.3, f32[128]{0:T(128)S(1)} %get-tuple-element.2), channel_id=1, replica_groups=mesh['sample'=4,'marker'=32] {'marker'}, use_global_device_ids=true, to_apply=%region_5.0 | all-reduce | flops 256 | bytes 2048 | tf_op jit(solution)/shard_map/psum | solution.py:54
  518.7 2.2 multiply_reduce_fusion.1
  520.9 66.8 %psum.91 = f32[128]{0:T(128)S(1)} all-reduce(f32[128]{0:T(128)S(1)} %multiply_reduce_fusion.1), channel_id=1, replica_groups=mesh['sample'=4,'marker'=32] {'marker'}, use_global_device_ids=true, to_apply=%region_11.0 | all-reduce | flops 128 | bytes 1024 | tf_op jit(solution)/shard_map/psum | solution.py:65
  587.7 3.6 multiply_add_fusion.1
  591.3 12.1 %fusion.1 = f32[128,2048]{1,0:T(8,128)S(1)} fusion(bf16[2048,4096]{1,0:T(8,128)(2,1)} %param.8, f32[128,4096]{1,0:T(8,128)} %multiply_add_fusion.1), kind=kOutput, calls=%fused_computation.11 | convolution fusion | flops 2148007936 | bytes 19922944 | tf_op jit(solution)/shard_map/dot_general | solution.py:17
  603.4 129.5 %all-reduce.17 = bf16[128,2048]{1,0:T(8,128)(2,1)} all-reduce(f32[128,2048]{1,0:T(8,128)S(1)} %fusion.1), channel_id=1, replica_groups=mesh['sample'=4,'marker'=32] {'marker'}, use_global_device_ids=true, to_apply=%region_12.0 | all-reduce | flops 262144 | bytes 1572864 | tf_op jit(solution)/shard_map/psum | solution.py:24
  732.9 9.6 %fusion.23 = f32[128,4096]{1,0:T(8,128)} fusion(bf16[128,2048]{1,0:T(8,128)(2,1)} %all-reduce.17, bf16[2048,4096]{1,0:T(8,128)(2,1)} %param.8), kind=kOutput, calls=%fused_computation.51 | convolution fusion | flops 2147483648 | bytes 19398656 | tf_op jit(solution)/shard_map/dot_general | solution.py:29
  742.5 0.0 all-reduce.15.cloned.1.call-update
  742.5 0.1 slice.18
  742.6 0.1 reshape.48
  742.7 58.7 %all-reduce.15.cloned.1.call-done = f32[128,4096]{1,0:T(8,128)} async-done(((f32[128,4096]{1,0:T(8,128)}), f32[128,4096]{1,0:T(8,128)}) %all-reduce.15.cloned.1.call-update) | async-done | bytes 2097168 | tf_op jit(solution)/shard_map/psum | solution.py:58
  801.3 2.7 multiply_reduce_fusion
  804.1 62.9 %psum.94 = f32[128]{0:T(128)S(1)} all-reduce(f32[128]{0:T(128)S(1)} %multiply_reduce_fusion), channel_id=1, replica_groups=mesh['sample'=4,'marker'=32] {'marker'}, use_global_device_ids=true, to_apply=%region_15.0 | all-reduce | flops 128 | bytes 1024 | tf_op jit(solution)/shard_map/psum | solution.py:60
  866.9 2.0 multiply_add_fusion
  868.9 0.0 copy-start.1
  868.9 1.3 copy-done.1
  870.3 0.0 copy-start.4
  870.3 0.0 copy-start.5
  870.3 0.0 copy-start.2
  870.3 0.3 fusion
  870.5 0.1 reshape.47
  870.7 66.8 %psum.95 = f32[16]{0:T(128)S(1)} all-reduce(f32[16]{0:T(128)S(1)} %reduce_sum.78), channel_id=1, replica_groups=mesh['sample'=4,'marker'=32] {'marker'}, use_global_device_ids=true, to_apply=%region_18.0 | all-reduce | flops 16 | bytes 128 | tf_op jit(solution)/shard_map/psum | solution.py:73
  937.5 0.0 copy-done.4
  937.5 0.0 copy-done.5
  937.5 0.0 copy-done.2
  937.5 2.0 fusion.16
  (11 shorter events, 0.1 us)
Async XLA Ops:
  7.2 181.9 %all-reduce.9.cloned.1.call-start = ((), (), s32[]{:S(2)}) async-start(), calls=%async_computation | async-start | bytes 262144 | tf_op jit(solution)/shard_map/psum | solution.py:24
  75.4 113.7 %copy-start.3 = (f32[16,2048]{1,0:T(8,128)S(1)}, f32[16,2048]{1,0:T(8,128)}, u32[]{:S(2)}) copy-start(f32[16,2048]{1,0:T(8,128)} %param.9) | copy-start | bytes 393220
  86.3 111.6 %copy-start.6 = (f32[16]{0:T(128)S(1)}, f32[16]{0:T(128)}, u32[]{:S(2)}) copy-start(f32[16]{0:T(128)} %param.15) | copy-start | bytes 196
  86.3 152.5 %copy-start = (f32[112,4096]{1,0:T(8,128)S(1)}, f32[112,4096]{1,0:T(8,128)}, u32[]{:S(2)}) copy-start(f32[112,4096]{1,0:T(8,128)} %param.11) | copy-start | bytes 5505028
  86.4 151.4 %all-reduce.11.cloned.1.call-start = ((), (), s32[]{:S(2)}) async-start(), calls=%async_computation.1 | async-start | bytes 524288 | tf_op jit(solution)/shard_map/psum | solution.py:47
  197.9 255.7 %all-reduce.13.cloned.1.call-start = ((), (), s32[]{:S(2)}) async-start(), calls=%async_computation.2 | async-start | bytes 4194304 | tf_op jit(solution)/shard_map/psum | solution.py:58
  393.9 407.5 %all-reduce.15.cloned.1.call-start = ((), (), s32[]{:S(2)}) async-start(), calls=%async_computation.3 | async-start | bytes 4194304 | tf_op jit(solution)/shard_map/psum | solution.py:58
  868.9 1.4 copy-start.1
  870.3 67.2 %copy-start.4 = (f32[16]{0:T(128)S(1)}, f32[16]{0:T(128)}, u32[]{:S(2)}) copy-start(f32[16]{0:T(128)} %param.13) | copy-start | bytes 196
  870.3 67.2 %copy-start.5 = (f32[16]{0:T(128)S(1)}, f32[16]{0:T(128)}, u32[]{:S(2)}) copy-start(f32[16]{0:T(128)} %param.14) | copy-start | bytes 196
  870.3 67.2 %copy-start.2 = (f32[16,4096]{1,0:T(8,128)S(1)}, f32[16,4096]{1,0:T(8,128)}, u32[]{:S(2)}) copy-start(f32[16,4096]{1,0:T(8,128)} %param.10) | copy-start | bytes 786436
Sparse Core Ops, SparseCore 0:
  86.5 102.5 all-reduce.8
  198.1 39.6 all-reduce.10
  394.0 59.5 all-reduce.12
  742.6 58.6 all-reduce.14
where the time goes:
time: 947 us; the launch traced here: 946 us
  blocking collectives  587 us (62%)
  waiting for transfers between devices  261 us (28%)
  matrix products  62.4 us (7%)
  other arithmetic  20.5 us (2%)
  between operations  13.9 us (1%)
    psum x2, blocking collectives, project(): predicted = lax.psum(partial_value, 'marker')  264 us
    psum x2, waiting for transfers between devices, per_device(): back_sum = lax.psum(back_sum, 'sample')  118 us
    psum x1, waiting for transfers between devices, project(): predicted = lax.psum(partial_value, 'marker')  103 us
    psum x1, blocking collectives, per_device(): norm_next = lax.psum(jnp.sum(residual * residual, axis=1), 'marker')  66.8 us
    psum x1, blocking collectives, per_device(): probe_dot = lax.psum(probe_local, 'marker')  66.8 us
    psum x1, blocking collectives, per_device(): first_slope = lax.psum(jnp.sum(slopes, axis=1), 'marker') / MARKERS  63.8 us
    psum x1, blocking collectives, per_device(): curvature = lax.psum(jnp.sum(direction * applied, axis=1), 'marker')  62.9 us
    psum x1, blocking collectives, per_device(): norm_start = lax.psum(jnp.sum(residual * residual, axis=1), 'marker')  62.9 us
  transfers between devices with their start and end apart: 4, of which 4 were waited for; matrix products, arithmetic and copies ran while one was open for 0% of the time, Pallas kernels for 0%

commit v1 on v0

--- a/solution.py
+++ b/solution.py
@@ -70,7 +70,11 @@
     probe_local = jnp.sum(
         jnp.sum(probes * iterate[traits:], axis=1).reshape(copies - 1, traits), axis=0
     )
-    probe_dot = lax.psum(probe_local, "marker")
+    probe_dot = probe_local
+    for hop in (1, 2, 4, 8, 16):
+        probe_dot = probe_dot + lax.ppermute(
+            probe_dot, "marker", [(dev, dev ^ hop) for dev in range(32)]
+        )
     probe_norm = jnp.sum(norm_start[traits:].reshape(copies - 1, traits), axis=0)
     second_slope = second_precision * probe_dot / (probe_norm + 1e-06)
     next_precision = second_precision * (1.0 - second_slope) / second_slope

time: 947 us -> 902 us (0.952)
  blocking collectives: 587 us -> 520 us
  waiting for transfers between devices: 261 us -> 274 us
    psum x1 -> x0, blocking collectives: 66.8 us -> none  [per_device(): probe_dot = lax.psum(probe_local, 'marker')]
    ppermute x0 -> x5, waiting for transfers between devices: none -> 13.3 us  [per_device(): lax.ppermute(probe_dot, 'marker', [(dev, dev ^ hop) for dev in range(32)])]
  transfers between devices with their start and end apart: 4 -> 9, of which waited for: 4 -> 9; matrix products, arithmetic and copies ran while one was open for 0% -> 0% of each run, Pallas kernels for 0% -> 0%
where the time goes in v1:
time: 902 us; the launch traced here: 898 us
  blocking collectives  520 us (58%)
  waiting for transfers between devices  274 us (30%)
  matrix products  62.4 us (7%)
  other arithmetic  20.5 us (2%)
  between operations  13.9 us (2%)
    psum x2, blocking collectives, project(): predicted = lax.psum(partial_value, 'marker')  264 us
    psum x2, waiting for transfers between devices, per_device(): back_sum = lax.psum(back_sum, 'sample')  118 us
    psum x1, waiting for transfers between devices, project(): predicted = lax.psum(partial_value, 'marker')  103 us
    psum x1, blocking collectives, per_device(): norm_next = lax.psum(jnp.sum(residual * residual, axis=1), 'marker')  66.8 us
    psum x1, blocking collectives, per_device(): first_slope = lax.psum(jnp.sum(slopes, axis=1), 'marker') / MARKERS  63.8 us
    psum x1, blocking collectives, per_device(): curvature = lax.psum(jnp.sum(direction * applied, axis=1), 'marker')  63.1 us
    psum x1, blocking collectives, per_device(): norm_start = lax.psum(jnp.sum(residual * residual, axis=1), 'marker')  62.9 us
    psum x1, waiting for transfers between devices, per_device(): start_back = lax.psum(start_back, 'sample')  39.8 us
  transfers between devices with their start and end apart: 9, of which 9 were waited for; matrix products, arithmetic and copies ran while one was open for 0% of the time, Pallas kernels for 0%

profile of v1, /device:TPU:1, one launch (start us, length us, event | category | flops | bytes accessed | tf_op | source)
XLA Modules:
  0.0 897.8 jit_solution(2404356652519607993)
XLA Ops:
  7.2 0.0 all-reduce.9.cloned.1.call-start
  7.2 0.7 multiply_add_fusion.4
  7.9 0.7 mul.192
  8.6 1.3 multiply_reduce_fusion.4
  9.8 63.8 %psum.77 = f32[16]{0:T(128)S(1)} all-reduce(f32[16]{0:T(128)S(1)} %multiply_reduce_fusion.4), channel_id=1, replica_groups=mesh['sample'=4,'marker'=32] {'marker'}, use_global_device_ids=true, to_apply=%region_1.0 | all-reduce | flops 16 | bytes 128 | tf_op jit(solution)/shard_map/psum | solution.py:43
  73.6 0.7 multiply_divide_fusion.1
  74.3 1.1 subtract_divide_fusion
  75.4 0.0 copy-start.3
  75.4 10.9 %fusion.17 = f32[16,2048]{1,0:T(8,128)} fusion(bf16[2048,4096]{1,0:T(8,128)(2,1)} %param.8, f32[16,4096]{1,0:T(8,128)S(1)} %subtract_divide_fusion), kind=kOutput, calls=%fused_computation.33 | convolution fusion | flops 268500992 | bytes 17170432 | tf_op jit(solution)/shard_map/dot_general | solution.py:17
  86.3 0.0 all-reduce.9.cloned.1.call-update
  86.3 0.0 copy-start.6
  86.3 0.0 copy-start
  86.4 0.0 all-reduce.11.cloned.1.call-start
  86.4 102.7 %all-reduce.9.cloned.1.call-done = f32[16,2048]{1,0:T(8,128)} async-done(((f32[16,2048]{1,0:T(8,128)}), f32[16,2048]{1,0:T(8,128)}) %all-reduce.9.cloned.1.call-update) | async-done | bytes 131088 | tf_op jit(solution)/shard_map/psum | solution.py:24
  189.1 0.0 copy-done.3
  189.1 8.8 fusion.19
  197.9 0.0 all-reduce.11.cloned.1.call-update
  197.9 0.0 all-reduce.13.cloned.1.call-start
  198.0 0.0 copy-done.6
  198.0 39.8 %all-reduce.11.cloned.1.call-done = f32[16,4096]{1,0:T(8,128)} async-done(((f32[16,4096]{1,0:T(8,128)}), f32[16,4096]{1,0:T(8,128)}) %all-reduce.11.cloned.1.call-update) | async-done | bytes 262160 | tf_op jit(solution)/shard_map/psum | solution.py:47
  237.8 1.0 broadcast_multiply_fusion
  238.8 0.0 copy-done
  238.8 11.4 %fusion.3 = f32[128,2048]{1,0:T(8,128)S(1)} fusion(bf16[2048,4096]{1,0:T(8,128)(2,1)} %param.8, f32[112,4096]{1,0:T(8,128)S(1)} %copy-done, f32[16,4096]{1,0:T(8,128)S(1)} %broadcast_multiply_fusion), kind=kOutput, calls=%fused_computation.13 | convolution fusion | flops 2149580800 | bytes 19922944 | tf_op jit(solution)/shard_map/dot_general | solution.py:17
  250.2 134.0 %all-reduce.16 = bf16[128,2048]{1,0:T(8,128)(2,1)} all-reduce(f32[128,2048]{1,0:T(8,128)S(1)} %fusion.3), channel_id=1, replica_groups=mesh['sample'=4,'marker'=32] {'marker'}, use_global_device_ids=true, to_apply=%region_6.0 | all-reduce | flops 262144 | bytes 1572864 | tf_op jit(solution)/shard_map/psum | solution.py:24
  384.2 9.6 %fusion.24 = f32[128,4096]{1,0:T(8,128)} fusion(bf16[128,2048]{1,0:T(8,128)(2,1)} %all-reduce.16, bf16[2048,4096]{1,0:T(8,128)(2,1)} %param.8), kind=kOutput, calls=%fused_computation.53 | convolution fusion | flops 2147483648 | bytes 19398656 | tf_op jit(solution)/shard_map/dot_general | solution.py:29
  393.9 0.0 all-reduce.13.cloned.1.call-update
  393.9 0.0 all-reduce.15.cloned.1.call-start
  394.0 0.1 mul.210
  394.0 0.1 mul.207
  394.1 59.5 %all-reduce.13.cloned.1.call-done = f32[128,4096]{1,0:T(8,128)} async-done(((f32[128,4096]{1,0:T(8,128)}), f32[128,4096]{1,0:T(8,128)}) %all-reduce.13.cloned.1.call-update) | async-done | bytes 2097168 | tf_op jit(solution)/shard_map/psum | solution.py:58
  453.6 2.2 multiply_reduce_fusion.2
  455.8 62.9 %all-reduce.1 = (f32[128]{0:T(128)S(1)}, f32[128]{0:T(128)S(1)}) all-reduce(f32[128]{0:T(128)S(1)} %get-tuple-element.3, f32[128]{0:T(128)S(1)} %get-tuple-element.2), channel_id=1, replica_groups=mesh['sample'=4,'marker'=32] {'marker'}, use_global_device_ids=true, to_apply=%region_5.0 | all-reduce | flops 256 | bytes 2048 | tf_op jit(solution)/shard_map/psum | solution.py:54
  518.7 2.2 multiply_reduce_fusion.1
  520.9 66.8 %psum.84 = f32[128]{0:T(128)S(1)} all-reduce(f32[128]{0:T(128)S(1)} %multiply_reduce_fusion.1), channel_id=1, replica_groups=mesh['sample'=4,'marker'=32] {'marker'}, use_global_device_ids=true, to_apply=%region_11.0 | all-reduce | flops 128 | bytes 1024 | tf_op jit(solution)/shard_map/psum | solution.py:65
  587.7 3.6 multiply_add_fusion.1
  591.3 12.1 %fusion.1 = f32[128,2048]{1,0:T(8,128)S(1)} fusion(bf16[2048,4096]{1,0:T(8,128)(2,1)} %param.8, f32[128,4096]{1,0:T(8,128)} %multiply_add_fusion.1), kind=kOutput, calls=%fused_computation.11 | convolution fusion | flops 2148007936 | bytes 19922944 | tf_op jit(solution)/shard_map/dot_general | solution.py:17
  603.4 129.5 %all-reduce.17 = bf16[128,2048]{1,0:T(8,128)(2,1)} all-reduce(f32[128,2048]{1,0:T(8,128)S(1)} %fusion.1), channel_id=1, replica_groups=mesh['sample'=4,'marker'=32] {'marker'}, use_global_device_ids=true, to_apply=%region_12.0 | all-reduce | flops 262144 | bytes 1572864 | tf_op jit(solution)/shard_map/psum | solution.py:24
  732.9 9.6 %fusion.23 = f32[128,4096]{1,0:T(8,128)} fusion(bf16[128,2048]{1,0:T(8,128)(2,1)} %all-reduce.17, bf16[2048,4096]{1,0:T(8,128)(2,1)} %param.8), kind=kOutput, calls=%fused_computation.52 | convolution fusion | flops 2147483648 | bytes 19398656 | tf_op jit(solution)/shard_map/dot_general | solution.py:29
  742.5 0.0 all-reduce.15.cloned.1.call-update
  742.5 58.8 %all-reduce.15.cloned.1.call-done = f32[128,4096]{1,0:T(8,128)} async-done(((f32[128,4096]{1,0:T(8,128)}), f32[128,4096]{1,0:T(8,128)}) %all-reduce.15.cloned.1.call-update) | async-done | bytes 2097168 | tf_op jit(solution)/shard_map/psum | solution.py:58
  801.3 2.7 multiply_reduce_fusion
  804.1 63.1 %psum.87 = f32[128]{0:T(128)S(1)} all-reduce(f32[128]{0:T(128)S(1)} %multiply_reduce_fusion), channel_id=1, replica_groups=mesh['sample'=4,'marker'=32] {'marker'}, use_global_device_ids=true, to_apply=%region_15.0 | all-reduce | flops 128 | bytes 1024 | tf_op jit(solution)/shard_map/psum | solution.py:60
  867.2 2.0 multiply_add_fusion
  869.1 0.0 copy-start.1
  869.2 1.3 copy-done.1
  870.5 0.0 copy-start.4
  870.5 0.3 fusion
  870.8 0.1 reshape.47
  870.9 4.9 collective-permute-start
  875.7 0.8 collective-permute-done
  876.5 0.0 collective-permute-start.1
  876.5 2.4 collective-permute-done.1
  879.0 0.0 collective-permute-start.2
  879.0 0.1 slice.18
  879.0 3.8 collective-permute-done.2
  882.9 0.0 collective-permute-start.3
  882.9 0.1 reshape.48
  883.0 2.3 collective-permute-done.3
  885.3 0.0 collective-permute-start.4
  885.3 3.9 collective-permute-done.4
  889.2 0.0 copy-done.4
  889.2 0.0 copy-done.5
  889.3 0.0 copy-done.2
  889.3 2.0 fusion.16
  (17 shorter events, 0.1 us)
Async XLA Ops:
  7.2 181.9 %all-reduce.9.cloned.1.call-start = ((), (), s32[]{:S(2)}) async-start(), calls=%async_computation | async-start | bytes 262144 | tf_op jit(solution)/shard_map/psum | solution.py:24
  75.4 113.7 %copy-start.3 = (f32[16,2048]{1,0:T(8,128)S(1)}, f32[16,2048]{1,0:T(8,128)}, u32[]{:S(2)}) copy-start(f32[16,2048]{1,0:T(8,128)} %param.9) | copy-start | bytes 393220
  86.3 111.6 %copy-start.6 = (f32[16]{0:T(128)S(1)}, f32[16]{0:T(128)}, u32[]{:S(2)}) copy-start(f32[16]{0:T(128)} %param.15) | copy-start | bytes 196
  86.3 152.5 %copy-start = (f32[112,4096]{1,0:T(8,128)S(1)}, f32[112,4096]{1,0:T(8,128)}, u32[]{:S(2)}) copy-start(f32[112,4096]{1,0:T(8,128)} %param.11) | copy-start | bytes 5505028
  86.4 151.4 %all-reduce.11.cloned.1.call-start = ((), (), s32[]{:S(2)}) async-start(), calls=%async_computation.1 | async-start | bytes 524288 | tf_op jit(solution)/shard_map/psum | solution.py:47
  197.9 255.7 %all-reduce.13.cloned.1.call-start = ((), (), s32[]{:S(2)}) async-start(), calls=%async_computation.2 | async-start | bytes 4194304 | tf_op jit(solution)/shard_map/psum | solution.py:58
  393.9 407.5 %all-reduce.15.cloned.1.call-start = ((), (), s32[]{:S(2)}) async-start(), calls=%async_computation.3 | async-start | bytes 4194304 | tf_op jit(solution)/shard_map/psum | solution.py:58
  869.1 1.4 copy-start.1
  870.5 18.8 %copy-start.4 = (f32[16]{0:T(128)S(1)}, f32[16]{0:T(128)}, u32[]{:S(2)}) copy-start(f32[16]{0:T(128)} %param.13) | copy-start | bytes 196
  870.5 18.8 %copy-start.5 = (f32[16]{0:T(128)S(1)}, f32[16]{0:T(128)}, u32[]{:S(2)}) copy-start(f32[16]{0:T(128)} %param.14) | copy-start | bytes 196
  870.5 18.8 %copy-start.2 = (f32[16,4096]{1,0:T(8,128)S(1)}, f32[16,4096]{1,0:T(8,128)}, u32[]{:S(2)}) copy-start(f32[16,4096]{1,0:T(8,128)} %param.10) | copy-start | bytes 786436
  870.9 5.7 collective-permute-start
  876.5 2.4 collective-permute-start.1
  879.0 3.9 collective-permute-start.2
  882.9 2.4 collective-permute-start.3
  885.3 3.9 collective-permute-start.4
Sparse Core Ops, SparseCore 0:
  86.5 102.5 all-reduce.8
  198.1 39.6 all-reduce.10
  394.0 59.5 all-reduce.12
  742.6 58.6 all-reduce.14
